TPU v7x, 128 devices: a whole 4x4x4 slice. The times are simulated.
128 devices in a mesh: pool: 2 (over core), grp: 4 (over y), rep: 16 (over x, z).
Axes of the slice: x: 4, y: 4, z: 4, core: 2. Of those that a mesh axis runs over, the one named last changes fastest.
Arguments:
- queries: bfloat16 [512, 8192], P('pool', 'grp'), may hold values from -64 to 64
- keys: bfloat16 [16384, 512], P('rep', 'grp'), may hold values from -7 to 7
- values: bfloat16 [16384, 512], P('rep', 'grp'), may hold values from -6 to 6
- hidden_in: bfloat16 [512, 4096], P(('pool', 'grp', 'rep')), may hold values from -4 to 4
- o_weight: bfloat16 [8192, 4096], P('grp', 'rep'), may hold values from -0.125 to 0.125
- norm_gain: bfloat16 [4096], replicated, may hold values from 0.5 to 1.5
- routes: int32 [512, 8], P(('pool', 'grp', 'rep')), may hold values from 0 to 63, as said below
- route_weights: float32 [512, 8], P(('pool', 'grp', 'rep')), may hold values from 0.02 to 0.25
- w_gate: bfloat16 [64, 4096, 1536], P(('grp', 'rep'), None, 'pool'), may hold values from -0.09375 to 0.09375
- w_up: bfloat16 [64, 4096, 1536], P(('grp', 'rep'), None, 'pool'), may hold values from -0.09375 to 0.09375
- w_down: bfloat16 [64, 1536, 4096], P(('grp', 'rep'), 'pool'), may hold values from -0.15625 to 0.15625
Outputs:
- mid_rows: bfloat16 [512, 4096], P(('pool', 'grp', 'rep'))
- expert_mix: bfloat16 [512, 4096], P(('pool', 'grp', 'rep'))
Inputs may be any that keep to these rules, and one draw needn't show every extreme that they name: `routes`: each row names 8 different experts. In the rows of one device each expert is named by no row or by exactly 2 rows, and one expert, the same on every device, is named by 2 rows on every device.
All inputs are finite; a program needn't handle non-finite values.
Results may differ from a plain program's by a relative error of at most 0.027.
Values may be sent and summed in bfloat16 or wider, within the bound.
A program may use at most 128 MiB of HBM per device.

v0:
```python
import jax
import jax.numpy as jnp
from jax import lax
from jax.sharding import PartitionSpec as P

HEAD_DIM = 128


def expert_apply(rows_in, gate_w, up_w, down_w):
    gate_proj = jnp.dot(rows_in, gate_w, preferred_element_type=jnp.float32)
    upper = jnp.dot(rows_in, up_w, preferred_element_type=jnp.float32)
    activated = (jax.nn.silu(gate_proj) * upper).astype(jnp.bfloat16)
    return jnp.dot(activated, down_w, preferred_element_type=jnp.float32)


def per_device(
    queries,
    keys,
    values,
    hidden_in,
    o_weight,
    norm_gain,
    routes,
    route_weights,
    w_gate,
    w_up,
    w_down,
):
    kv_local = keys.shape[1] // HEAD_DIM
    heads_local = queries.shape[1] // HEAD_DIM
    group_size = heads_local // kv_local
    batch_rows = queries.shape[0]
    key_span = keys.shape[0]
    per_block = min(4, group_size)
    blocks = group_size // per_block
    score_scale = HEAD_DIM ** (-0.5)
    query_blocks = jnp.moveaxis(
        queries.reshape(batch_rows, kv_local, blocks, per_block, HEAD_DIM), 2, 0
    )
    key_heads = keys.reshape(key_span, kv_local, HEAD_DIM)
    value_heads = values.reshape(key_span, kv_local, HEAD_DIM)

    def local_part(query_block):
        scores = (
            jnp.einsum("rkhd,pkd->rkhp", query_block, key_heads, preferred_element_type=jnp.float32)
            * score_scale
        )
        top_score = jnp.max(scores, axis=-1)
        exp_scores = jnp.exp(scores - top_score[..., None])
        exp_total = jnp.sum(exp_scores, axis=-1)
        weighted = jnp.einsum(
            "rkhp,pkd->rkhd",
            exp_scores.astype(jnp.bfloat16),
            value_heads,
            preferred_element_type=jnp.float32,
        )
        return (top_score, exp_total, weighted)

    top_part, total_part, value_part = lax.map(local_part, query_blocks)
    rep_size = lax.axis_size("rep")
    share = batch_rows // rep_size
    rows_heads = share * heads_local

    def by_peer(part):
        part = jnp.moveaxis(part, 0, 2)
        return part.reshape((rep_size, rows_heads) + part.shape[4:])

    stats = jnp.stack([by_peer(top_part), by_peer(total_part)], axis=1)
    payload = jnp.concatenate([by_peer(value_part), stats.reshape(rep_size, -1, HEAD_DIM)], axis=1)
    payload = lax.all_to_all(payload, "rep", split_axis=0, concat_axis=0, tiled=True)
    weighted = payload[:, :rows_heads]
    stats = payload[:, rows_heads:].reshape(rep_size, 2, rows_heads)
    joint_top = jnp.max(stats[:, 0], axis=0)
    factors = jnp.exp(stats[:, 0] - joint_top)
    exp_total = jnp.sum(stats[:, 1] * factors, axis=0)
    weighted = jnp.sum(weighted * factors[..., None], axis=0)
    attention = (weighted / exp_total[:, None]).astype(jnp.bfloat16)
    attention = lax.all_gather(
        attention.reshape(share, heads_local * HEAD_DIM), "rep", axis=0, tiled=True
    )
    head_total = lax.psum_scatter(
        jnp.dot(attention, o_weight, preferred_element_type=jnp.float32),
        "grp",
        scatter_dimension=0,
        tiled=True,
    )
    attn_proj = head_total.astype(jnp.bfloat16)
    full_rows = lax.all_to_all(attn_proj, "rep", split_axis=0, concat_axis=1, tiled=True)
    mid_rows = (hidden_in.astype(jnp.float32) + full_rows.astype(jnp.float32)).astype(jnp.bfloat16)
    mid_wide = lax.optimization_barrier(mid_rows).astype(jnp.float32)
    inverse = lax.rsqrt(jnp.mean(mid_wide * mid_wide, axis=-1, keepdims=True) + 1e-06)
    normed = (mid_wide * inverse * norm_gain.astype(jnp.float32)).astype(jnp.bfloat16)
    row_dev, topk = routes.shape
    model_width = hidden_in.shape[1]
    group_count = lax.axis_size("grp")
    rep_count = lax.axis_size("rep")
    experts = group_count * rep_count
    capacity = max(2, 2 * row_dev * topk // experts)
    flat_routes = routes.reshape(-1)
    order = jnp.arange(flat_routes.shape[0], dtype=jnp.int32)
    same_before = (flat_routes[:, None] == flat_routes[None, :]) & (order[None, :] < order[:, None])
    position = jnp.sum(same_before.astype(jnp.int32), axis=1)
    slot_index = flat_routes * capacity + position
    chooser = jnp.any(
        jnp.arange(experts * capacity, dtype=jnp.int32)[:, None, None]
        == slot_index.reshape(row_dev, topk)[None, :, :],
        axis=2,
    ).astype(jnp.bfloat16)
    outgoing = jnp.dot(chooser, normed, preferred_element_type=jnp.float32).astype(jnp.bfloat16)
    arrived = lax.all_to_all(
        outgoing.reshape(experts, capacity, model_width),
        ("grp", "rep"),
        split_axis=0,
        concat_axis=0,
        tiled=True,
    )
    sources = arrived.shape[0]
    slots_here = arrived.shape[1]
    combined = expert_apply(
        lax.all_gather(arrived.reshape(-1, model_width), "pool", axis=0, tiled=True),
        w_gate[0],
        w_up[0],
        w_down[0],
    )
    served = (
        lax.psum_scatter(combined, "pool", scatter_dimension=0, tiled=True)
        .astype(jnp.bfloat16)
        .reshape(sources, slots_here, model_width)
    )
    returned = lax.all_to_all(served, ("grp", "rep"), split_axis=0, concat_axis=0, tiled=True)
    returned = returned.reshape(-1, model_width)
    picked = jnp.take(returned, slot_index, axis=0).reshape(row_dev, topk, model_width)
    expert_mix = jnp.sum(route_weights[..., None] * picked.astype(jnp.float32), axis=1).astype(
        jnp.bfloat16
    )
    return (mid_rows, expert_mix)


def solution(mesh):
    return jax.shard_map(
        per_device,
        mesh=mesh,
        in_specs=(
            P("pool", "grp"),
            P("rep", "grp"),
            P("rep", "grp"),
            P(("pool", "grp", "rep"), None),
            P("grp", "rep"),
            P(),
            P(("pool", "grp", "rep"), None),
            P(("pool", "grp", "rep"), None),
            P(("grp", "rep"), None, "pool"),
            P(("grp", "rep"), None, "pool"),
            P(("grp", "rep"), "pool", None),
        ),
        out_specs=(P(("pool", "grp", "rep"), None), P(("pool", "grp", "rep"), None)),
        check_vma=False,
    )
```

profile of v0, /device:TPU:0, one launch (start us, length us, event | category | flops | bytes accessed | tf_op | source)
XLA Modules:
  0.0 256.5 jit_solution(1512416310897008572)
XLA Ops:
  7.2 0.0 copy-start
  7.2 0.0 all-gather.3.cloned.1.call-start
  7.3 1.6 copy.23
  8.8 17.8 %while.14 = (s32[]{:T(128)}, f32[4,256,1,4]{1,3,2,0:T(4,128)S(1)}, f32[4,256,1,4]{1,3,2,0:T(4,128)S(1)}, f32[4,256,1,4,128]{4,1,3,2,0:T(8,128)}, bf16[4,256,1,4,...) while((s32[]{:T(128)}, f32[4,256,1,4]{1,3,2,0:T(4,128)S(1)}, ...), condition=%wide.region_3.4_spmd, body=%wide.region_0.3_spmd.sunk | while | flops 545257472 | bytes 14975609 | solution.py:59
  8.8 1.8 bitcast_reduce_fusion.2
  10.7 0.9 fusion.67
  11.6 1.6 fusion.68
  13.3 1.8 bitcast_reduce_fusion.2
  15.1 0.9 fusion.67
  16.0 1.7 fusion.68
  17.7 1.8 bitcast_reduce_fusion.2
  19.5 0.9 fusion.67
  20.5 1.7 fusion.68
  22.1 1.8 bitcast_reduce_fusion.2
  23.9 0.9 fusion.67
  24.9 1.7 fusion.68
  26.6 0.3 copy.26
  26.8 0.5 stack_reshape.6
  27.3 0.3 copy.27
  27.6 0.5 stack_reshape.7
  28.2 2.9 %copy.25 = f32[256,1,4,4,128]{4,3,2,0,1:T(4,128)S(1)} copy(f32[256,1,4,4,128]{4,0,3,1,2:T(8,128)} %bitcast.21) | data formatting | bytes 4194304 | tf_op jit(solution)/shard_map/transpose | solution.py:65
  31.1 0.2 pad_maximum_fusion
  31.3 0.0 copy-start.4
  31.3 37.1 %all_to_all.28 = f32[16,260,128]{2,1,0:T(8,128)S(1)} all-to-all(f32[16,260,128]{2,1,0:T(8,128)S(1)} %pad_maximum_fusion), channel_id=1, replica_groups=mesh['pool'=2,'grp'=4,'rep'=16] {'rep'}, dimensions={0} | all-to-all | bytes 4259840 | tf_op jit(solution)/shard_map/all_to_all | solution.py:70
  68.5 0.7 fusion.27
  69.3 0.1 div.20
  69.3 0.1 div.21
  69.4 0.7 fusion.37
  70.1 0.0 all-gather.3.cloned.1.call-update
  70.2 0.0 reduce-scatter.3.cloned.1.call-start
  70.2 40.9 %all-gather.3.cloned.1.call-done = bf16[256,2048]{1,0:T(8,128)(2,1)} async-done(((bf16[16,2048]{1,0:T(8,128)(2,1)}), bf16[256,2048]{1,0:T(8,128)(2,1)}) %all-gather.3.cloned.1.call-update) | async-done | bytes 1048592 | tf_op jit(solution)/shard_map/all_gather | solution.py:78
  111.1 2.4 fusion.55
  113.5 0.0 reduce-scatter.3.cloned.1.call-update
  113.5 0.1 reshape.156
  113.6 0.2 convert_reduce_fusion
  113.8 0.1 reduce_sum.64
  113.9 19.6 %reduce-scatter.3.cloned.1.call-done = f32[64,256]{1,0:T(8,128)} async-done(((f32[256,256]{1,0:T(8,128)}), f32[64,256]{1,0:T(8,128)}) %reduce-scatter.3.cloned.1.call-update) | async-done | bytes 65552 | tf_op jit(solution)/shard_map/reduce_scatter | solution.py:81
  133.5 0.8 convert_element_type.55
  134.4 0.6 all_to_all.20
  135.0 6.9 %all-to-all-start.1 = ((bf16[16,4,256]{2,1,0:T(4,128)(2,1)}), bf16[16,4,256]{2,1,0:T(4,128)(2,1)S(1)}, u32[]{:S(2)}, u32[]{:S(2)}) async-start(bf16[16,4,256]{2,1,0:T(4,128)(2,1)} %all_to_all.20), calls=%async_computation.2 | async-start | bytes 65536 | tf_op jit(solution)/shard_map/all_to_all | solution.py:88
  142.0 0.0 all-gather.5.cloned.1.call-start
  142.0 0.1 fusion.48
  142.1 7.5 %all-to-all-done.1 = bf16[16,4,256]{2,1,0:T(4,128)(2,1)S(1)} async-done(((bf16[16,4,256]{2,1,0:T(4,128)(2,1)}), bf16[16,4,256]{2,1,0:T(4,128)(2,1)S(1)}, u32[]{:S(2)}, u32[]{:S(2)}) %all-to-all-start.1) | async-done | bytes 32800 | tf_op jit(solution)/shard_map/all_to_all | solution.py:88
  149.6 0.0 copy-start.2
  149.6 0.1 fusion.38
  149.8 0.5 convolution_convert_fusion
  150.3 0.7 reshape.157
  151.0 20.0 %all_to_all.29 = bf16[64,2,4096]{2,1,0:T(2,128)(2,1)S(1)} all-to-all(bf16[64,2,4096]{2,1,0:T(2,128)(2,1)S(1)} %reshape.157), channel_id=1, replica_groups=mesh['pool'=2,'grp'=4,'rep'=16] {'grp','rep'}, dimensions={0} | all-to-all | bytes 2097152 | tf_op jit(solution)/shard_map/all_to_all | solution.py:110
  171.0 1.2 reshape.158
  172.2 0.0 all-gather.5.cloned.1.call-update
  172.3 0.2 reduce-scatter.5.cloned.1.call-start
  172.5 8.8 %all-gather.5.cloned.1.call-done = bf16[256,4096]{1,0:T(8,128)(2,1)} async-done(((bf16[128,4096]{1,0:T(8,128)(2,1)}), bf16[256,4096]{1,0:T(8,128)(2,1)}) %all-gather.5.cloned.1.call-update) | async-done | bytes 2097168 | tf_op jit(solution)/shard_map/all_gather | solution.py:120
  181.3 6.2 %fusion.25 = f32[256,768]{1,0:T(8,128)} fusion(bf16[256,4096]{1,0:T(8,128)(2,1)} %all-gather.5.cloned.1.call-done, bf16[1,4096,768]{2,1,0:T(8,128)(2,1)} %param.21), kind=kOutput, calls=%fused_computation.25 | convolution fusion | flops 1610612736 | bytes 9175040 | tf_op jit(solution)/shard_map/dot_general | solution.py:10
  187.5 11.3 %fusion.21 = f32[256,4096]{1,0:T(8,128)} fusion(bf16[1,768,4096]{2,1,0:T(8,128)(2,1)} %param.23, bf16[256,4096]{1,0:T(8,128)(2,1)S(1)} %copy-done.7, bf16[1,4096,768]{2,1,0:T(8,128)(2,1)} %param.22, f32[256,768]{1,0:T(8,128)} %fusion.25), kind=kOutput, calls=%fused_computation.21 | convolution fusion | flops 3222405120 | bytes 19660800 | tf_op jit(solution)/shard_map/dot_general | solution.py:13
  198.9 0.0 reduce-scatter.5.cloned.1.call-update
  198.9 16.4 %reduce-scatter.5.cloned.1.call-done = f32[128,4096]{1,0:T(8,128)} async-done(((f32[256,4096]{1,0:T(8,128)}), f32[128,4096]{1,0:T(8,128)}) %reduce-scatter.5.cloned.1.call-update) | async-done | bytes 2097168 | tf_op jit(solution)/shard_map/reduce_scatter | solution.py:126
  215.2 1.7 convert_element_type.66
  217.0 1.5 reshape.159
  218.5 10.4 %all-to-all-start.3 = ((bf16[64,2,4096]{2,1,0:T(2,128)(2,1)}), bf16[64,2,4096]{2,1,0:T(2,128)(2,1)S(1)}, u32[]{:S(2)}, u32[]{:S(2)}) async-start(bf16[64,2,4096]{2,1,0:T(2,128)(2,1)} %reshape.159), calls=%async_computation.5 | async-start | bytes 2097152 | tf_op jit(solution)/shard_map/all_to_all | solution.py:130
  228.9 0.1 mul.91
  229.0 18.9 %all-to-all-done.3 = bf16[64,2,4096]{2,1,0:T(2,128)(2,1)S(1)} async-done(((bf16[64,2,4096]{2,1,0:T(2,128)(2,1)}), bf16[64,2,4096]{2,1,0:T(2,128)(2,1)S(1)}, u32[]{:S(2)}, u32[]{:S(2)}) %all-to-all-start.3) | async-done | bytes 1048608 | tf_op jit(solution)/shard_map/all_to_all | solution.py:130
  247.9 0.4 reshape.160
  248.4 0.7 gather_fusion
  249.1 0.9 multiply_reduce_fusion
  (42 shorter events, 0.4 us)
Async XLA Ops:
  7.2 104.0 %copy-start = (bf16[2048,256]{1,0:T(8,128)(2,1)S(1)}, bf16[2048,256]{1,0:T(8,128)(2,1)}, u32[]{:S(2)}) copy-start(bf16[2048,256]{1,0:T(8,128)(2,1)} %param.17) | copy-start | bytes 3145732
  7.2 103.9 %all-gather.3.cloned.1.call-start = ((), (), s32[]{:S(2)}) async-start(), calls=%async_computation.6 | async-start | bytes 1114112 | tf_op jit(solution)/shard_map/all_gather | solution.py:78
  8.8 2.8 %copy-start.1 = (bf16[1024,1,128]{2,0,1:T(8,128)(2,1)S(1)}, bf16[1024,1,128]{2,0,1:T(8,128)(2,1)}, u32[]{:S(2)}) copy-start(bf16[1024,1,128]{2,0,1:T(8,128)(2,1)} %get-tuple-element.156) | copy-start | bytes 786436 | tf_op jit(solution)/shard_map/while
  13.3 2.8 %copy-start.1 = (bf16[1024,1,128]{2,0,1:T(8,128)(2,1)S(1)}, bf16[1024,1,128]{2,0,1:T(8,128)(2,1)}, u32[]{:S(2)}) copy-start(bf16[1024,1,128]{2,0,1:T(8,128)(2,1)} %get-tuple-element.156) | copy-start | bytes 786436 | tf_op jit(solution)/shard_map/while
  17.7 2.8 %copy-start.1 = (bf16[1024,1,128]{2,0,1:T(8,128)(2,1)S(1)}, bf16[1024,1,128]{2,0,1:T(8,128)(2,1)}, u32[]{:S(2)}) copy-start(bf16[1024,1,128]{2,0,1:T(8,128)(2,1)} %get-tuple-element.156) | copy-start | bytes 786436 | tf_op jit(solution)/shard_map/while
  22.1 2.8 %copy-start.1 = (bf16[1024,1,128]{2,0,1:T(8,128)(2,1)S(1)}, bf16[1024,1,128]{2,0,1:T(8,128)(2,1)}, u32[]{:S(2)}) copy-start(bf16[1024,1,128]{2,0,1:T(8,128)(2,1)} %get-tuple-element.156) | copy-start | bytes 786436 | tf_op jit(solution)/shard_map/while
  31.3 82.3 %copy-start.4 = (s32[4,8]{1,0:T(4,128)S(1)}, s32[4,8]{1,0:T(4,128)}, u32[]{:S(2)}) copy-start(s32[4,8]{1,0:T(4,128)} %param.19) | copy-start | bytes 388
  31.3 110.8 %copy-start.5 = (bf16[4096]{0:T(1024)(128)(2,1)S(1)}, bf16[4096]{0:T(1024)(128)(2,1)}, u32[]{:S(2)}) copy-start(bf16[4096]{0:T(1024)(128)(2,1)} %param.18) | copy-start | bytes 24580
  68.4 81.2 %copy-start.3 = (bf16[4,4096]{1,0:T(4,128)(2,1)S(1)}, bf16[4,4096]{1,0:T(4,128)(2,1)}, u32[]{:S(2)}) copy-start(bf16[4,4096]{1,0:T(4,128)(2,1)} %param.16) | copy-start | bytes 98308
  70.2 63.4 %reduce-scatter.3.cloned.1.call-start = ((), (), s32[]{:S(2)}) async-start(), calls=%async_computation.7 | async-start | bytes 327680 | tf_op jit(solution)/shard_map/reduce_scatter | solution.py:81
  135.0 14.6 %all-to-all-start.1 = ((bf16[16,4,256]{2,1,0:T(4,128)(2,1)}), bf16[16,4,256]{2,1,0:T(4,128)(2,1)S(1)}, u32[]{:S(2)}, u32[]{:S(2)}) async-start(bf16[16,4,256]{2,1,0:T(4,128)(2,1)} %all_to_all.20), calls=%async_computation.2 | async-start | bytes 65536 | tf_op jit(solution)/shard_map/all_to_all | solution.py:88
  142.0 39.4 %all-gather.5.cloned.1.call-start = ((), (), s32[]{:S(2)}) async-start(), calls=%async_computation.8 | async-start | bytes 3145728 | tf_op jit(solution)/shard_map/all_gather | solution.py:120
  149.6 22.6 %copy-start.2 = (bf16[4,4096]{1,0:T(4,128)(2,1)}, bf16[4,4096]{1,0:T(4,128)(2,1)S(1)}, u32[]{:S(2)}) copy-start(bf16[4,4096]{1,0:T(4,128)(2,1)S(1)} %add_convert_fusion) | copy-start | bytes 98308
  172.3 43.0 %reduce-scatter.5.cloned.1.call-start = ((), (), s32[]{:S(2)}) async-start(), calls=%async_computation.9 | async-start | bytes 6291456 | tf_op jit(solution)/shard_map/reduce_scatter | solution.py:126
  181.3 6.2 %copy-start.7 = (bf16[256,4096]{1,0:T(8,128)(2,1)S(1)}, bf16[256,4096]{1,0:T(8,128)(2,1)}, u32[]{:S(2)}) copy-start(bf16[256,4096]{1,0:T(8,128)(2,1)} %all-gather.5.cloned.1.call-done) | copy-start | bytes 6291460
  217.0 32.1 %copy-start.6 = (f32[4,8]{1,0:T(4,128)S(1)}, f32[4,8]{1,0:T(4,128)}, u32[]{:S(2)}) copy-start(f32[4,8]{1,0:T(4,128)} %param.20) | copy-start | bytes 388
  218.5 29.4 %all-to-all-start.3 = ((bf16[64,2,4096]{2,1,0:T(2,128)(2,1)}), bf16[64,2,4096]{2,1,0:T(2,128)(2,1)S(1)}, u32[]{:S(2)}, u32[]{:S(2)}) async-start(bf16[64,2,4096]{2,1,0:T(2,128)(2,1)} %reshape.159), calls=%async_computation.5 | async-start | bytes 2097152 | tf_op jit(solution)/shard_map/all_to_all | solution.py:130
Sparse Core Ops, SparseCore 0:
  70.3 40.8 all-gather.2
  113.6 19.8 reduce-scatter.2
  172.4 8.9 all-gather.4
  199.0 16.1 reduce-scatter.4
where the time goes:
time: 257 us; the launch traced here: 256 us
  waiting for transfers between devices  112 us (44%)
  blocking collectives  57.1 us (22%)
  matrix products  34.3 us (13%)
  starting transfers between devices  17.7 us (7%)
  between operations  14 us (5%)
  local copies, waits for them, and re-layouts  11.9 us (5%)
  other arithmetic  9.24 us (4%)
    all_gather x1, waiting for transfers between devices, per_device(): lax.all_gather(attention.reshape(share, heads_local * HEAD_DIM), 'rep', a...  40.9 us
    all_to_all x1, blocking collectives, per_device(): lax.all_to_all(payload, 'rep', split_axis=0, concat_axis=0, tiled=True)  37.1 us
    all_to_all x1, blocking collectives, per_device(): lax.all_to_all(outgoing.reshape(experts, capacity, model_width), ('grp',...  20 us
    reduce_scatter x1, waiting for transfers between devices, per_device(): lax.psum_scatter(jnp.dot(attention, o_weight, preferred_element_type=jnp....  19.6 us
    all_to_all x1, waiting for transfers between devices, per_device(): lax.all_to_all(served, ('grp', 'rep'), split_axis=0, concat_axis=0, tiled...  18.9 us
    reduce_scatter x1, waiting for transfers between devices, per_device(): lax.psum_scatter(combined, 'pool', scatter_dimension=0, tiled=True)  16.4 us
    dot_general x1, matrix products, expert_apply(): return jnp.dot(activated, down_w, preferred_element_type=jnp.float32)  11.3 us
    all_to_all x1, starting transfers between devices, per_device(): lax.all_to_all(served, ('grp', 'rep'), split_axis=0, concat_axis=0, tiled...  10.4 us
  transfers between devices with their start and end apart: 6, of which 6 were waited for; matrix products, arithmetic and copies ran while one was open for 0% of the time, Pallas kernels for 0%

commit v1 on v0

--- a/solution.py
+++ b/solution.py
@@ -75,9 +75,20 @@
     exp_total = jnp.sum(stats[:, 1] * factors, axis=0)
     weighted = jnp.sum(weighted * factors[..., None], axis=0)
     attention = (weighted / exp_total[:, None]).astype(jnp.bfloat16)
-    attention = lax.all_gather(
-        attention.reshape(share, heads_local * HEAD_DIM), "rep", axis=0, tiled=True
-    )
+    x = attention.reshape(share, heads_local * HEAD_DIM)
+    ways, here, step = (lax.axis_size("rep"), lax.axis_index("rep"), x.shape[0])
+    dims = [n * ways if d == 0 else n for d, n in enumerate(x.shape)]
+    full = lax.dynamic_update_slice_in_dim(jnp.zeros(dims, x.dtype), x, here * step, axis=0)
+    going_up = going_down = x
+    for far in range(1, ways // 2 + 1):
+        going_up = lax.ppermute(going_up, "rep", [(d, (d + 1) % ways) for d in range(ways)])
+        full = lax.dynamic_update_slice_in_dim(full, going_up, (here - far) % ways * step, axis=0)
+        if 2 * far < ways:
+            going_down = lax.ppermute(going_down, "rep", [(d, (d - 1) % ways) for d in range(ways)])
+            full = lax.dynamic_update_slice_in_dim(
+                full, going_down, (here + far) % ways * step, axis=0
+            )
+    attention = full
     head_total = lax.psum_scatter(
         jnp.dot(attention, o_weight, preferred_element_type=jnp.float32),
         "grp",

time: 257 us -> 276 us (1.074)
  starting transfers between devices: 17.7 us -> 64 us
  blocking collectives: 57.1 us -> 20 us
  waiting for transfers between devices: 112 us -> 122 us
    all_gather x1 -> x0, waiting for transfers between devices: 40.9 us -> none  [per_device(): lax.all_gather(attention.reshape(share, heads_local * HEAD_DIM), 'rep', a...]
    ppermute x0 -> x15, starting transfers between devices: none -> 38.6 us  [the longest x7 38 us: per_device(): lax.ppermute(going_down, 'rep', [(d, (d - 1) % ways) for d in range(ways)])]
    all_to_all x1 -> x0, blocking collectives: 37.1 us -> none  [per_device(): lax.all_to_all(payload, 'rep', split_axis=0, concat_axis=0, tiled=True)]
    all_to_all x0 -> x1, waiting for transfers between devices: none -> 31.1 us  [per_device(): lax.all_to_all(payload, 'rep', split_axis=0, concat_axis=0, tiled=True)]
    ppermute x0 -> x15, waiting for transfers between devices: none -> 22.3 us  [the longest x8 22.3 us: per_device(): lax.ppermute(going_up, 'rep', [(d, (d + 1) % ways) for d in range(ways)])]
    all_to_all x0 -> x1, starting transfers between devices: none -> 7.96 us  [per_device(): lax.all_to_all(payload, 'rep', split_axis=0, concat_axis=0, tiled=True)]
    reduce_scatter x1, waiting for transfers between devices: 19.6 us -> 16.8 us  [per_device(): lax.psum_scatter(jnp.dot(attention, o_weight, preferred_element_type=jnp....]
  transfers between devices with their start and end apart: 6 -> 21, of which waited for: 6 -> 14; matrix products, arithmetic and copies ran while one was open for 0% -> 0% of each run, Pallas kernels for 0% -> 0%
where the time goes in v1:
time: 276 us; the launch traced here: 275 us
  waiting for transfers between devices  122 us (44%)
  starting transfers between devices  64 us (23%)
  matrix products  33.1 us (12%)
  blocking collectives  20 us (7%)
  between operations  14.1 us (5%)
  local copies, waits for them, and re-layouts  12.1 us (4%)
  other arithmetic  9.97 us (4%)
    ppermute x7, starting transfers between devices, per_device(): lax.ppermute(going_down, 'rep', [(d, (d - 1) % ways) for d in range(ways)])  38 us
    all_to_all x1, waiting for transfers between devices, per_device(): lax.all_to_all(payload, 'rep', split_axis=0, concat_axis=0, tiled=True)  31.1 us
    ppermute x8, waiting for transfers between devices, per_device(): lax.ppermute(going_up, 'rep', [(d, (d + 1) % ways) for d in range(ways)])  22.3 us
    all_to_all x1, blocking collectives, per_device(): lax.all_to_all(outgoing.reshape(experts, capacity, model_width), ('grp',...  20 us
    all_to_all x1, waiting for transfers between devices, per_device(): lax.all_to_all(served, ('grp', 'rep'), split_axis=0, concat_axis=0, tiled...  18.9 us
    reduce_scatter x1, waiting for transfers between devices, per_device(): lax.psum_scatter(jnp.dot(attention, o_weight, preferred_element_type=jnp....  16.8 us
    reduce_scatter x1, waiting for transfers between devices, per_device(): lax.psum_scatter(combined, 'pool', scatter_dimension=0, tiled=True)  16.4 us
    dot_general x1, matrix products, expert_apply(): return jnp.dot(activated, down_w, preferred_element_type=jnp.float32)  11.3 us
  transfers between devices with their start and end apart: 21, of which 14 were waited for; matrix products, arithmetic and copies ran while one was open for 0% of the time, Pallas kernels for 0%

profile of v1, /device:TPU:0, one launch (start us, length us, event | category | flops | bytes accessed | tf_op | source)
XLA Modules:
  0.0 275.5 jit_solution(17222109291386911689)
XLA Ops:
  7.2 1.6 copy.23
  8.8 17.7 %while.14 = (s32[]{:T(128)}, f32[4,256,1,4]{1,3,2,0:T(4,128)S(1)}, f32[4,256,1,4]{1,3,2,0:T(4,128)S(1)}, f32[4,256,1,4,128]{4,1,3,2,0:T(8,128)}, bf16[4,256,1,4,...) while((s32[]{:T(128)}, f32[4,256,1,4]{1,3,2,0:T(4,128)S(1)}, ...), condition=%wide.region_3.4_spmd, body=%wide.region_0.3_spmd.sunk | while | flops 545257472 | bytes 14975609 | solution.py:59
  8.8 1.8 bitcast_reduce_fusion.2
  10.6 0.9 fusion.68
  11.6 1.7 fusion.69
  13.2 1.8 bitcast_reduce_fusion.2
  15.0 0.9 fusion.68
  16.0 1.7 fusion.69
  17.6 1.8 bitcast_reduce_fusion.2
  19.5 0.9 fusion.68
  20.4 1.7 fusion.69
  22.1 1.8 bitcast_reduce_fusion.2
  23.9 0.9 fusion.68
  24.9 1.7 fusion.69
  26.5 0.3 copy.26
  26.8 0.5 stack_reshape.6
  27.3 0.3 copy.27
  27.5 0.5 stack_reshape.7
  28.1 2.9 %copy.25 = f32[256,1,4,4,128]{4,3,2,0,1:T(4,128)S(1)} copy(f32[256,1,4,4,128]{4,0,3,1,2:T(8,128)} %bitcast.21) | data formatting | bytes 4194304 | tf_op jit(solution)/shard_map/transpose | solution.py:65
  31.1 1.5 pad_maximum_fusion
  32.6 8.0 %all-to-all-start = ((f32[16,260,128]{2,1,0:T(8,128)}), f32[16,260,128]{2,1,0:T(8,128)S(1)}, u32[]{:S(2)}, u32[]{:S(2)}) async-start(f32[16,260,128]{2,1,0:T(8,128)} %pad_maximum_fusion), calls=%async_computation | async-start | bytes 4325376 | tf_op jit(solution)/shard_map/all_to_all | solution.py:70
  40.6 31.1 %all-to-all-done = f32[16,260,128]{2,1,0:T(8,128)S(1)} async-done(((f32[16,260,128]{2,1,0:T(8,128)}), f32[16,260,128]{2,1,0:T(8,128)S(1)}, u32[]{:S(2)}, u32[]{:S(2)}) %all-to-all-start) | async-done | bytes 2129952 | tf_op jit(solution)/shard_map/all_to_all | solution.py:70
  71.9 0.7 fusion.27
  72.7 0.1 div.21
  72.8 0.1 broadcast_in_dim.37
  73.0 0.6 collective-permute-start
  73.6 4.8 %collective-permute-start.1 = (bf16[16,2048]{1,0:T(8,128)(2,1)S(1)}, bf16[16,2048]{1,0:T(8,128)(2,1)S(1)}, u32[]{:S(2)}, u32[]{:S(2)}) collective-permute-start(bf16[16,2048]{1,0:T(8,128)(2,1)S(1)} %get-tuple-element.75), channel_id=1, source_target_pairs={{0,15},{1,0},{2,1},{3,2},{4,3},{5,4},{6,5},{7,6},{8,7},{9,8},{10,9... | collective-permute-start | bytes 196616 | tf_op jit(solution)/shard_map/ppermute | solution.py:87
  78.4 2.2 collective-permute-done
  80.7 5.3 %collective-permute-start.3 = (bf16[16,2048]{1,0:T(8,128)(2,1)S(1)}, bf16[16,2048]{1,0:T(8,128)(2,1)S(1)}, u32[]{:S(2)}, u32[]{:S(2)}) collective-permute-start(bf16[16,2048]{1,0:T(8,128)(2,1)S(1)} %collective-permute-done.1), channel_id=1, source_target_pairs={{0,15},{1,0},{2,1},{3,2},{4,3},{5,4},{6,5},{7,6},{8,7},{9,8},{10,9... | collective-permute-start | bytes 196616 | tf_op jit(solution)/shard_map/ppermute | solution.py:87
  86.0 2.2 collective-permute-done.2
  88.3 5.3 %collective-permute-start.5 = (bf16[16,2048]{1,0:T(8,128)(2,1)S(1)}, bf16[16,2048]{1,0:T(8,128)(2,1)S(1)}, u32[]{:S(2)}, u32[]{:S(2)}) collective-permute-start(bf16[16,2048]{1,0:T(8,128)(2,1)S(1)} %collective-permute-done.3), channel_id=1, source_target_pairs={{0,15},{1,0},{2,1},{3,2},{4,3},{5,4},{6,5},{7,6},{8,7},{9,8},{10,9... | collective-permute-start | bytes 196616 | tf_op jit(solution)/shard_map/ppermute | solution.py:87
  93.6 2.6 collective-permute-done.4
  96.2 5.6 %collective-permute-start.7 = (bf16[16,2048]{1,0:T(8,128)(2,1)S(1)}, bf16[16,2048]{1,0:T(8,128)(2,1)S(1)}, u32[]{:S(2)}, u32[]{:S(2)}) collective-permute-start(bf16[16,2048]{1,0:T(8,128)(2,1)S(1)} %collective-permute-done.5), channel_id=1, source_target_pairs={{0,15},{1,0},{2,1},{3,2},{4,3},{5,4},{6,5},{7,6},{8,7},{9,8},{10,9... | collective-permute-start | bytes 196616 | tf_op jit(solution)/shard_map/ppermute | solution.py:87
  101.9 1.9 collective-permute-done.6
  103.8 5.6 %collective-permute-start.9 = (bf16[16,2048]{1,0:T(8,128)(2,1)S(1)}, bf16[16,2048]{1,0:T(8,128)(2,1)S(1)}, u32[]{:S(2)}, u32[]{:S(2)}) collective-permute-start(bf16[16,2048]{1,0:T(8,128)(2,1)S(1)} %collective-permute-done.7), channel_id=1, source_target_pairs={{0,15},{1,0},{2,1},{3,2},{4,3},{5,4},{6,5},{7,6},{8,7},{9,8},{10,9... | collective-permute-start | bytes 196616 | tf_op jit(solution)/shard_map/ppermute | solution.py:87
  109.4 1.9 collective-permute-done.8
  111.4 5.6 %collective-permute-start.11 = (bf16[16,2048]{1,0:T(8,128)(2,1)S(1)}, bf16[16,2048]{1,0:T(8,128)(2,1)S(1)}, u32[]{:S(2)}, u32[]{:S(2)}) collective-permute-start(bf16[16,2048]{1,0:T(8,128)(2,1)S(1)} %collective-permute-done.9), channel_id=1, source_target_pairs={{0,15},{1,0},{2,1},{3,2},{4,3},{5,4},{6,5},{7,6},{8,7},{9,8},{10,9... | collective-permute-start | bytes 196616 | tf_op jit(solution)/shard_map/ppermute | solution.py:87
  117.0 1.9 collective-permute-done.10
  119.0 5.6 %collective-permute-start.13 = (bf16[16,2048]{1,0:T(8,128)(2,1)S(1)}, bf16[16,2048]{1,0:T(8,128)(2,1)S(1)}, u32[]{:S(2)}, u32[]{:S(2)}) collective-permute-start(bf16[16,2048]{1,0:T(8,128)(2,1)S(1)} %collective-permute-done.11), channel_id=1, source_target_pairs={{0,15},{1,0},{2,1},{3,2},{4,3},{5,4},{6,5},{7,6},{8,7},{9,8},{10,9... | collective-permute-start | bytes 196616 | tf_op jit(solution)/shard_map/ppermute | solution.py:87
  124.6 1.9 collective-permute-done.12
  126.6 7.5 %collective-permute-done.14 = bf16[16,2048]{1,0:T(8,128)(2,1)S(1)} collective-permute-done((bf16[16,2048]{1,0:T(8,128)(2,1)S(1)}, bf16[16,2048]{1,0:T(8,128)(2,1)S(1)}, u32[]{:S(2)}, u32[]{:S(2)}) %collective-permute-start.14) | collective-permute-done | bytes 65568 | tf_op jit(solution)/shard_map/ppermute | solution.py:84
  134.2 1.1 fusion.56
  135.4 0.2 convert_reduce_fusion
  135.7 16.8 %reduce-scatter.3.cloned.1.call-done = f32[64,256]{1,0:T(8,128)} async-done(((f32[256,256]{1,0:T(8,128)}), f32[64,256]{1,0:T(8,128)}) %reduce-scatter.3.cloned.1.call-update) | async-done | bytes 65552 | tf_op jit(solution)/shard_map/reduce_scatter | solution.py:92
  152.5 0.8 convert_element_type.55
  153.4 0.6 all_to_all.20
  154.0 6.9 %all-to-all-start.1 = ((bf16[16,4,256]{2,1,0:T(4,128)(2,1)}), bf16[16,4,256]{2,1,0:T(4,128)(2,1)S(1)}, u32[]{:S(2)}, u32[]{:S(2)}) async-start(bf16[16,4,256]{2,1,0:T(4,128)(2,1)} %all_to_all.20), calls=%async_computation.2 | async-start | bytes 65536 | tf_op jit(solution)/shard_map/all_to_all | solution.py:99
  161.1 7.5 %all-to-all-done.1 = bf16[16,4,256]{2,1,0:T(4,128)(2,1)S(1)} async-done(((bf16[16,4,256]{2,1,0:T(4,128)(2,1)}), bf16[16,4,256]{2,1,0:T(4,128)(2,1)S(1)}, u32[]{:S(2)}, u32[]{:S(2)}) %all-to-all-start.1) | async-done | bytes 32800 | tf_op jit(solution)/shard_map/all_to_all | solution.py:99
  168.6 0.1 fusion.38
  168.8 0.5 convolution_convert_fusion
  169.3 0.7 reshape.157
  170.0 20.0 %all_to_all.28 = bf16[64,2,4096]{2,1,0:T(2,128)(2,1)S(1)} all-to-all(bf16[64,2,4096]{2,1,0:T(2,128)(2,1)S(1)} %reshape.157), channel_id=1, replica_groups=mesh['pool'=2,'grp'=4,'rep'=16] {'grp','rep'}, dimensions={0} | all-to-all | bytes 2097152 | tf_op jit(solution)/shard_map/all_to_all | solution.py:121
  190.0 1.2 reshape.158
  191.3 9.0 %all-gather.2.cloned.1.call-done = bf16[256,4096]{1,0:T(8,128)(2,1)} async-done(((bf16[128,4096]{1,0:T(8,128)(2,1)}), bf16[256,4096]{1,0:T(8,128)(2,1)}) %all-gather.2.cloned.1.call-update) | async-done | bytes 2097168 | tf_op jit(solution)/shard_map/all_gather | solution.py:131
  200.3 6.2 %fusion.25 = f32[256,768]{1,0:T(8,128)} fusion(bf16[256,4096]{1,0:T(8,128)(2,1)} %all-gather.2.cloned.1.call-done, bf16[1,4096,768]{2,1,0:T(8,128)(2,1)} %param.21), kind=kOutput, calls=%fused_computation.25 | convolution fusion | flops 1610612736 | bytes 9175040 | tf_op jit(solution)/shard_map/dot_general | solution.py:10
  206.5 11.3 %fusion.21 = f32[256,4096]{1,0:T(8,128)} fusion(bf16[1,768,4096]{2,1,0:T(8,128)(2,1)} %param.23, bf16[256,4096]{1,0:T(8,128)(2,1)S(1)} %copy-done.7, bf16[1,4096,768]{2,1,0:T(8,128)(2,1)} %param.22, f32[256,768]{1,0:T(8,128)} %fusion.25), kind=kOutput, calls=%fused_computation.21 | convolution fusion | flops 3222405120 | bytes 19660800 | tf_op jit(solution)/shard_map/dot_general | solution.py:13
  217.9 16.4 %reduce-scatter.5.cloned.1.call-done = f32[128,4096]{1,0:T(8,128)} async-done(((f32[256,4096]{1,0:T(8,128)}), f32[128,4096]{1,0:T(8,128)}) %reduce-scatter.5.cloned.1.call-update) | async-done | bytes 2097168 | tf_op jit(solution)/shard_map/reduce_scatter | solution.py:137
  234.2 1.7 convert_element_type.66
  236.0 1.5 reshape.159
  237.5 10.4 %all-to-all-start.3 = ((bf16[64,2,4096]{2,1,0:T(2,128)(2,1)}), bf16[64,2,4096]{2,1,0:T(2,128)(2,1)S(1)}, u32[]{:S(2)}, u32[]{:S(2)}) async-start(bf16[64,2,4096]{2,1,0:T(2,128)(2,1)} %reshape.159), calls=%async_computation.5 | async-start | bytes 2097152 | tf_op jit(solution)/shard_map/all_to_all | solution.py:141
  248.0 18.9 %all-to-all-done.3 = bf16[64,2,4096]{2,1,0:T(2,128)(2,1)S(1)} async-done(((bf16[64,2,4096]{2,1,0:T(2,128)(2,1)}), bf16[64,2,4096]{2,1,0:T(2,128)(2,1)S(1)}, u32[]{:S(2)}, u32[]{:S(2)}) %all-to-all-start.3) | async-done | bytes 1048608 | tf_op jit(solution)/shard_map/all_to_all | solution.py:141
  266.9 0.4 reshape.160
  267.4 0.7 gather_fusion
  268.1 0.9 multiply_reduce_fusion
  (86 shorter events, 1.2 us)
Async XLA Ops:
  7.2 127.0 %copy-start = (bf16[2048,256]{1,0:T(8,128)(2,1)S(1)}, bf16[2048,256]{1,0:T(8,128)(2,1)}, u32[]{:S(2)}) copy-start(bf16[2048,256]{1,0:T(8,128)(2,1)} %param.17) | copy-start | bytes 3145732
  8.8 2.8 %copy-start.1 = (bf16[1024,1,128]{2,0,1:T(8,128)(2,1)S(1)}, bf16[1024,1,128]{2,0,1:T(8,128)(2,1)}, u32[]{:S(2)}) copy-start(bf16[1024,1,128]{2,0,1:T(8,128)(2,1)} %get-tuple-element.158) | copy-start | bytes 786436 | tf_op jit(solution)/shard_map/while
  13.2 2.8 %copy-start.1 = (bf16[1024,1,128]{2,0,1:T(8,128)(2,1)S(1)}, bf16[1024,1,128]{2,0,1:T(8,128)(2,1)}, u32[]{:S(2)}) copy-start(bf16[1024,1,128]{2,0,1:T(8,128)(2,1)} %get-tuple-element.158) | copy-start | bytes 786436 | tf_op jit(solution)/shard_map/while
  17.6 2.8 %copy-start.1 = (bf16[1024,1,128]{2,0,1:T(8,128)(2,1)S(1)}, bf16[1024,1,128]{2,0,1:T(8,128)(2,1)}, u32[]{:S(2)}) copy-start(bf16[1024,1,128]{2,0,1:T(8,128)(2,1)} %get-tuple-element.158) | copy-start | bytes 786436 | tf_op jit(solution)/shard_map/while
  22.1 2.8 %copy-start.1 = (bf16[1024,1,128]{2,0,1:T(8,128)(2,1)S(1)}, bf16[1024,1,128]{2,0,1:T(8,128)(2,1)}, u32[]{:S(2)}) copy-start(bf16[1024,1,128]{2,0,1:T(8,128)(2,1)} %get-tuple-element.158) | copy-start | bytes 786436 | tf_op jit(solution)/shard_map/while
  32.6 39.2 %all-to-all-start = ((f32[16,260,128]{2,1,0:T(8,128)}), f32[16,260,128]{2,1,0:T(8,128)S(1)}, u32[]{:S(2)}, u32[]{:S(2)}) async-start(f32[16,260,128]{2,1,0:T(8,128)} %pad_maximum_fusion), calls=%async_computation | async-start | bytes 4325376 | tf_op jit(solution)/shard_map/all_to_all | solution.py:70
  40.5 112.0 %reduce-scatter.3.cloned.1.call-start = ((), (), s32[]{:S(2)}) async-start(), calls=%async_computation.6 | async-start | bytes 327680 | tf_op jit(solution)/shard_map/reduce_scatter | solution.py:92
  71.9 63.5 %copy-start.4 = (s32[4,8]{1,0:T(4,128)S(1)}, s32[4,8]{1,0:T(4,128)}, u32[]{:S(2)}) copy-start(s32[4,8]{1,0:T(4,128)} %param.19) | copy-start | bytes 388
  71.9 89.2 %copy-start.5 = (bf16[4096]{0:T(1024)(128)(2,1)S(1)}, bf16[4096]{0:T(1024)(128)(2,1)}, u32[]{:S(2)}) copy-start(bf16[4096]{0:T(1024)(128)(2,1)} %param.18) | copy-start | bytes 24580
  72.6 96.0 %copy-start.3 = (bf16[4,4096]{1,0:T(4,128)(2,1)S(1)}, bf16[4,4096]{1,0:T(4,128)(2,1)}, u32[]{:S(2)}) copy-start(bf16[4,4096]{1,0:T(4,128)(2,1)} %param.16) | copy-start | bytes 98308
  73.0 7.7 %collective-permute-start = (bf16[16,2048]{1,0:T(8,128)(2,1)S(1)}, bf16[16,2048]{1,0:T(8,128)(2,1)S(1)}, u32[]{:S(2)}, u32[]{:S(2)}) collective-permute-start(bf16[16,2048]{1,0:T(8,128)(2,1)S(1)} %get-tuple-element.75), channel_id=1, source_target_pairs={{0,1},{1,2},{2,3},{3,4},{4,5},{5,6},{6,7},{7,8},{8,9},{9,10},{10,1... | collective-permute-start | bytes 196616 | tf_op jit(solution)/shard_map/ppermute | solution.py:84
  73.6 7.0 %collective-permute-start.1 = (bf16[16,2048]{1,0:T(8,128)(2,1)S(1)}, bf16[16,2048]{1,0:T(8,128)(2,1)S(1)}, u32[]{:S(2)}, u32[]{:S(2)}) collective-permute-start(bf16[16,2048]{1,0:T(8,128)(2,1)S(1)} %get-tuple-element.75), channel_id=1, source_target_pairs={{0,15},{1,0},{2,1},{3,2},{4,3},{5,4},{6,5},{7,6},{8,7},{9,8},{10,9... | collective-permute-start | bytes 196616 | tf_op jit(solution)/shard_map/ppermute | solution.py:87
  80.7 7.6 %collective-permute-start.2 = (bf16[16,2048]{1,0:T(8,128)(2,1)S(1)}, bf16[16,2048]{1,0:T(8,128)(2,1)S(1)}, u32[]{:S(2)}, u32[]{:S(2)}) collective-permute-start(bf16[16,2048]{1,0:T(8,128)(2,1)S(1)} %collective-permute-done), channel_id=1, source_target_pairs={{0,1},{1,2},{2,3},{3,4},{4,5},{5,6},{6,7},{7,8},{8,9},{9,10},{10,1... | collective-permute-start | bytes 196616 | tf_op jit(solution)/shard_map/ppermute | solution.py:84
  80.7 7.6 %collective-permute-start.3 = (bf16[16,2048]{1,0:T(8,128)(2,1)S(1)}, bf16[16,2048]{1,0:T(8,128)(2,1)S(1)}, u32[]{:S(2)}, u32[]{:S(2)}) collective-permute-start(bf16[16,2048]{1,0:T(8,128)(2,1)S(1)} %collective-permute-done.1), channel_id=1, source_target_pairs={{0,15},{1,0},{2,1},{3,2},{4,3},{5,4},{6,5},{7,6},{8,7},{9,8},{10,9... | collective-permute-start | bytes 196616 | tf_op jit(solution)/shard_map/ppermute | solution.py:87
  88.2 8.0 %collective-permute-start.4 = (bf16[16,2048]{1,0:T(8,128)(2,1)S(1)}, bf16[16,2048]{1,0:T(8,128)(2,1)S(1)}, u32[]{:S(2)}, u32[]{:S(2)}) collective-permute-start(bf16[16,2048]{1,0:T(8,128)(2,1)S(1)} %collective-permute-done.2), channel_id=1, source_target_pairs={{0,1},{1,2},{2,3},{3,4},{4,5},{5,6},{6,7},{7,8},{8,9},{9,10},{10,1... | collective-permute-start | bytes 196616 | tf_op jit(solution)/shard_map/ppermute | solution.py:84
  88.3 8.0 %collective-permute-start.5 = (bf16[16,2048]{1,0:T(8,128)(2,1)S(1)}, bf16[16,2048]{1,0:T(8,128)(2,1)S(1)}, u32[]{:S(2)}, u32[]{:S(2)}) collective-permute-start(bf16[16,2048]{1,0:T(8,128)(2,1)S(1)} %collective-permute-done.3), channel_id=1, source_target_pairs={{0,15},{1,0},{2,1},{3,2},{4,3},{5,4},{6,5},{7,6},{8,7},{9,8},{10,9... | collective-permute-start | bytes 196616 | tf_op jit(solution)/shard_map/ppermute | solution.py:87
  96.2 7.6 %collective-permute-start.6 = (bf16[16,2048]{1,0:T(8,128)(2,1)S(1)}, bf16[16,2048]{1,0:T(8,128)(2,1)S(1)}, u32[]{:S(2)}, u32[]{:S(2)}) collective-permute-start(bf16[16,2048]{1,0:T(8,128)(2,1)S(1)} %collective-permute-done.4), channel_id=1, source_target_pairs={{0,1},{1,2},{2,3},{3,4},{4,5},{5,6},{6,7},{7,8},{8,9},{9,10},{10,1... | collective-permute-start | bytes 196616 | tf_op jit(solution)/shard_map/ppermute | solution.py:84
  96.2 7.6 %collective-permute-start.7 = (bf16[16,2048]{1,0:T(8,128)(2,1)S(1)}, bf16[16,2048]{1,0:T(8,128)(2,1)S(1)}, u32[]{:S(2)}, u32[]{:S(2)}) collective-permute-start(bf16[16,2048]{1,0:T(8,128)(2,1)S(1)} %collective-permute-done.5), channel_id=1, source_target_pairs={{0,15},{1,0},{2,1},{3,2},{4,3},{5,4},{6,5},{7,6},{8,7},{9,8},{10,9... | collective-permute-start | bytes 196616 | tf_op jit(solution)/shard_map/ppermute | solution.py:87
  103.8 7.6 %collective-permute-start.8 = (bf16[16,2048]{1,0:T(8,128)(2,1)S(1)}, bf16[16,2048]{1,0:T(8,128)(2,1)S(1)}, u32[]{:S(2)}, u32[]{:S(2)}) collective-permute-start(bf16[16,2048]{1,0:T(8,128)(2,1)S(1)} %collective-permute-done.6), channel_id=1, source_target_pairs={{0,1},{1,2},{2,3},{3,4},{4,5},{5,6},{6,7},{7,8},{8,9},{9,10},{10,1... | collective-permute-start | bytes 196616 | tf_op jit(solution)/shard_map/ppermute | solution.py:84
  103.8 7.6 %collective-permute-start.9 = (bf16[16,2048]{1,0:T(8,128)(2,1)S(1)}, bf16[16,2048]{1,0:T(8,128)(2,1)S(1)}, u32[]{:S(2)}, u32[]{:S(2)}) collective-permute-start(bf16[16,2048]{1,0:T(8,128)(2,1)S(1)} %collective-permute-done.7), channel_id=1, source_target_pairs={{0,15},{1,0},{2,1},{3,2},{4,3},{5,4},{6,5},{7,6},{8,7},{9,8},{10,9... | collective-permute-start | bytes 196616 | tf_op jit(solution)/shard_map/ppermute | solution.py:87
  111.4 7.6 %collective-permute-start.10 = (bf16[16,2048]{1,0:T(8,128)(2,1)S(1)}, bf16[16,2048]{1,0:T(8,128)(2,1)S(1)}, u32[]{:S(2)}, u32[]{:S(2)}) collective-permute-start(bf16[16,2048]{1,0:T(8,128)(2,1)S(1)} %collective-permute-done.8), channel_id=1, source_target_pairs={{0,1},{1,2},{2,3},{3,4},{4,5},{5,6},{6,7},{7,8},{8,9},{9,10},{10,1... | collective-permute-start | bytes 196616 | tf_op jit(solution)/shard_map/ppermute | solution.py:84
  111.4 7.6 %collective-permute-start.11 = (bf16[16,2048]{1,0:T(8,128)(2,1)S(1)}, bf16[16,2048]{1,0:T(8,128)(2,1)S(1)}, u32[]{:S(2)}, u32[]{:S(2)}) collective-permute-start(bf16[16,2048]{1,0:T(8,128)(2,1)S(1)} %collective-permute-done.9), channel_id=1, source_target_pairs={{0,15},{1,0},{2,1},{3,2},{4,3},{5,4},{6,5},{7,6},{8,7},{9,8},{10,9... | collective-permute-start | bytes 196616 | tf_op jit(solution)/shard_map/ppermute | solution.py:87
  119.0 7.6 %collective-permute-start.12 = (bf16[16,2048]{1,0:T(8,128)(2,1)S(1)}, bf16[16,2048]{1,0:T(8,128)(2,1)S(1)}, u32[]{:S(2)}, u32[]{:S(2)}) collective-permute-start(bf16[16,2048]{1,0:T(8,128)(2,1)S(1)} %collective-permute-done.10), channel_id=1, source_target_pairs={{0,1},{1,2},{2,3},{3,4},{4,5},{5,6},{6,7},{7,8},{8,9},{9,10},{10,1... | collective-permute-start | bytes 196616 | tf_op jit(solution)/shard_map/ppermute | solution.py:84
  119.0 7.6 %collective-permute-start.13 = (bf16[16,2048]{1,0:T(8,128)(2,1)S(1)}, bf16[16,2048]{1,0:T(8,128)(2,1)S(1)}, u32[]{:S(2)}, u32[]{:S(2)}) collective-permute-start(bf16[16,2048]{1,0:T(8,128)(2,1)S(1)} %collective-permute-done.11), channel_id=1, source_target_pairs={{0,15},{1,0},{2,1},{3,2},{4,3},{5,4},{6,5},{7,6},{8,7},{9,8},{10,9... | collective-permute-start | bytes 196616 | tf_op jit(solution)/shard_map/ppermute | solution.py:87
  126.5 7.6 %collective-permute-start.14 = (bf16[16,2048]{1,0:T(8,128)(2,1)S(1)}, bf16[16,2048]{1,0:T(8,128)(2,1)S(1)}, u32[]{:S(2)}, u32[]{:S(2)}) collective-permute-start(bf16[16,2048]{1,0:T(8,128)(2,1)S(1)} %collective-permute-done.12), channel_id=1, source_target_pairs={{0,1},{1,2},{2,3},{3,4},{4,5},{5,6},{6,7},{7,8},{8,9},{9,10},{10,1... | collective-permute-start | bytes 196616 | tf_op jit(solution)/shard_map/ppermute | solution.py:84
  154.0 14.6 %all-to-all-start.1 = ((bf16[16,4,256]{2,1,0:T(4,128)(2,1)}), bf16[16,4,256]{2,1,0:T(4,128)(2,1)S(1)}, u32[]{:S(2)}, u32[]{:S(2)}) async-start(bf16[16,4,256]{2,1,0:T(4,128)(2,1)} %all_to_all.20), calls=%async_computation.2 | async-start | bytes 65536 | tf_op jit(solution)/shard_map/all_to_all | solution.py:99
  160.9 39.3 %all-gather.2.cloned.1.call-start = ((), (), s32[]{:S(2)}) async-start(), calls=%async_computation.7 | async-start | bytes 3145728 | tf_op jit(solution)/shard_map/all_gather | solution.py:131
  168.6 22.6 %copy-start.2 = (bf16[4,4096]{1,0:T(4,128)(2,1)}, bf16[4,4096]{1,0:T(4,128)(2,1)S(1)}, u32[]{:S(2)}) copy-start(bf16[4,4096]{1,0:T(4,128)(2,1)S(1)} %add_convert_fusion) | copy-start | bytes 98308
  191.2 43.0 %reduce-scatter.5.cloned.1.call-start = ((), (), s32[]{:S(2)}) async-start(), calls=%async_computation.8 | async-start | bytes 6291456 | tf_op jit(solution)/shard_map/reduce_scatter | solution.py:137
  200.3 6.2 %copy-start.7 = (bf16[256,4096]{1,0:T(8,128)(2,1)S(1)}, bf16[256,4096]{1,0:T(8,128)(2,1)}, u32[]{:S(2)}) copy-start(bf16[256,4096]{1,0:T(8,128)(2,1)} %all-gather.2.cloned.1.call-done) | copy-start | bytes 6291460
  236.0 32.1 %copy-start.6 = (f32[4,8]{1,0:T(4,128)S(1)}, f32[4,8]{1,0:T(4,128)}, u32[]{:S(2)}) copy-start(f32[4,8]{1,0:T(4,128)} %param.20) | copy-start | bytes 388
  237.5 29.4 %all-to-all-start.3 = ((bf16[64,2,4096]{2,1,0:T(2,128)(2,1)}), bf16[64,2,4096]{2,1,0:T(2,128)(2,1)S(1)}, u32[]{:S(2)}, u32[]{:S(2)}) async-start(bf16[64,2,4096]{2,1,0:T(2,128)(2,1)} %reshape.159), calls=%async_computation.5 | async-start | bytes 2097152 | tf_op jit(solution)/shard_map/all_to_all | solution.py:141
Sparse Core Ops, SparseCore 0:
  135.4 17.0 reduce-scatter.2
  191.3 8.9 all-gather.1
  218.0 16.1 reduce-scatter.4
